TPU v7x, 32 devices: a whole 2x2x4 slice. The times are simulated.
32 devices in a mesh: parts: 1, node: 4 (over y, x), local: 8 (over z, core).
Axes of the slice: x: 2, y: 2, z: 4, core: 2. Of those that a mesh axis runs over, the one named last changes fastest.
Arguments:
- tokens: bfloat16 [2048, 4096], P(('parts', 'node', 'local')), may hold values from -6 to 6
- expert_ids: int32 [2048, 8], P(('parts', 'node', 'local')), may hold values from 0 to 15, all different within a row; in each aligned block of 64 rows (0 to 63, 64 to 127, ...) at most 40 rows name the same one
- gate_weights: float32 [2048, 8], P(('parts', 'node', 'local')), may hold values from 0.02 to 0.5
- w_gate: bfloat16 [4096, 12288], P(None, ('parts', 'node', 'local')), may hold values from -0.09375 to 0.09375
- w_up: bfloat16 [4096, 12288], P(None, ('parts', 'node', 'local')), may hold values from -0.09375 to 0.09375
- w_down: bfloat16 [12288, 4096], P(('parts', 'node', 'local')), may hold values from -0.21875 to 0.21875
Outputs:
- mixed: bfloat16 [2048, 4096], P(('parts', 'node', 'local'))
Inputs may be any that keep to these rules, and one draw needn't show every extreme that they name: `expert_ids`: each token names 8 different experts; among the 64 tokens of one device no expert is named more than 40 times, and in some such block one expert is named exactly 40 times.
All inputs are finite; a program needn't handle non-finite values.
Results may differ from a plain program's by a relative error of at most 0.0058.
Values may be sent and summed in bfloat16 or wider, within the bound.
A program may use at most 128 MiB of HBM per device.

v0:
```python
import jax
import jax.numpy as jnp
from jax import lax
from jax.sharding import PartitionSpec as P


def partner_2(value, axis, bit):
    mask = 2**bit
    pairs = [(source, source ^ mask) for source in range(lax.axis_size(axis))]
    return lax.ppermute(value, axis, pairs)


def per_device(tokens, expert_ids, gate_weights, w_gate, w_up, w_down):
    node_count = lax.axis_size("node")
    local_count = lax.axis_size("local")
    devices = node_count * local_count
    experts = devices // 2
    tok_rows, top_count = expert_ids.shape
    width = tokens.shape[1]
    capacity = tok_rows * top_count * 5 // (4 * experts)
    flat_ids = expert_ids.reshape(-1)
    one_hot = (flat_ids[:, None] == jnp.arange(experts, dtype=jnp.int32)[None, :]).astype(jnp.int32)
    earlier = jnp.cumsum(one_hot, axis=0) - one_hot
    slot_rank = jnp.sum(earlier * one_hot, axis=1)
    slot_index = (flat_ids * capacity + slot_rank).reshape(tok_rows, top_count)
    slot_table = jnp.any(
        slot_index[None, :, :] == jnp.arange(experts * capacity, dtype=jnp.int32)[:, None, None],
        axis=2,
    ).astype(jnp.bfloat16)
    outgoing = jnp.dot(slot_table, tokens, preferred_element_type=jnp.float32).astype(jnp.bfloat16)
    outgoing = outgoing.reshape(devices, capacity // 2, width)
    partner = partner_2((w_gate, w_up, w_down), "local", 0)
    full_gate = jnp.concatenate([w_gate, partner[0]], axis=1)
    full_up = jnp.concatenate([w_up, partner[1]], axis=1)
    full_down = jnp.concatenate([w_down, partner[2]], axis=0)
    block = lax.all_to_all(outgoing, ("node", "local"), split_axis=0, concat_axis=0, tiled=True)
    rows = block.reshape(-1, width)
    gate = jnp.dot(rows, full_gate, preferred_element_type=jnp.float32)
    upper = jnp.dot(rows, full_up, preferred_element_type=jnp.float32)
    hidden = (jax.nn.silu(gate) * upper).astype(jnp.bfloat16)
    result = jnp.dot(hidden, full_down, preferred_element_type=jnp.float32).astype(jnp.bfloat16)
    processed = result.reshape(block.shape)
    returned = lax.all_to_all(processed, ("node", "local"), split_axis=0, concat_axis=0, tiled=True)
    results = returned.reshape(experts * capacity, width)
    chosen = results[slot_index]
    mixed = jnp.sum(gate_weights[:, :, None] * chosen.astype(jnp.float32), axis=1)
    return mixed.astype(jnp.bfloat16)


def solution(mesh):
    placed = (
        P(("parts", "node", "local"), None),
        P(("parts", "node", "local"), None),
        P(("parts", "node", "local"), None),
        P(None, ("parts", "node", "local")),
        P(None, ("parts", "node", "local")),
        P(("parts", "node", "local"), None),
    )
    return jax.shard_map(
        per_device,
        mesh=mesh,
        in_specs=placed,
        out_specs=P(("parts", "node", "local"), None),
        check_vma=False,
    )
```

profile of v0, /device:TPU:10, one launch (start us, length us, event | category | flops | bytes accessed | tf_op | source)
XLA Modules:
  0.0 370.1 jit_solution(10786451935689527593)
XLA Ops:
  0.0 0.8 copy.22
  1.0 1.2 reduce-window.6
  2.2 0.2 slice_reduce_fusion
  2.4 0.1 fusion.20
  2.5 0.1 reduce_sum.21
  2.7 0.7 compare_select_fusion
  3.5 0.5 fusion.12
  4.0 3.9 %convolution_convert_fusion.1 = bf16[640,4096]{1,0:T(8,128)(2,1)} fusion(pred[640,64]{0,1:T(8,128)(4,1)S(1)} %fusion.12, bf16[64,4096]{1,0:T(8,128)(2,1)S(1)} %copy-done), kind=kOutput, calls=%fused_computation.4 | convolution fusion | flops 338165760 | bytes 5808128 | tf_op jit(solution)/shard_map/dot_general | solution.py:30
  7.9 7.6 %reshape.40 = bf16[32,20,4096]{2,1,0:T(8,128)(2,1)} reshape(bf16[640,4096]{1,0:T(8,128)(2,1)} %convolution_convert_fusion.1) | data formatting | bytes 10485760 | tf_op jit(solution)/shard_map/reshape | solution.py:31
  15.5 6.1 %all-to-all-start = ((bf16[32,20,4096]{2,1,0:T(8,128)(2,1)}), bf16[32,20,4096]{2,1,0:T(8,128)(2,1)}, u32[]{:S(2)}, u32[]{:S(2)}) async-start(bf16[32,20,4096]{2,1,0:T(8,128)(2,1)} %reshape.40), calls=%async_computation | async-start | bytes 12582912 | tf_op jit(solution)/shard_map/all_to_all | solution.py:36
  21.6 0.2 collective-permute-start.1
  21.7 0.4 collective-permute-start
  22.1 0.1 collective-permute-start.2
  22.2 134.8 %all-to-all-done = bf16[32,20,4096]{2,1,0:T(8,128)(2,1)} async-done(((bf16[32,20,4096]{2,1,0:T(8,128)(2,1)}), bf16[32,20,4096]{2,1,0:T(8,128)(2,1)}, u32[]{:S(2)}, u32[]{:S(2)}) %all-to-all-start) | async-done | bytes 5242912 | tf_op jit(solution)/shard_map/all_to_all | solution.py:36
  157.0 7.8 %reshape.41 = bf16[640,4096]{1,0:T(8,128)(2,1)} reshape(bf16[32,20,4096]{2,1,0:T(8,128)(2,1)} %all-to-all-done) | data formatting | bytes 10485760 | tf_op jit(solution)/shard_map/reshape | solution.py:37
  164.9 8.6 %fusion.5 = f32[640,768]{1,0:T(8,128)S(1)} fusion(bf16[640,4096]{1,0:T(8,128)(2,1)} %reshape.41, bf16[4096,384]{1,0:T(8,128)(2,1)} %collective-permute-done.1, bf16[4096,384]{1,0:T(8,128)(2,1)} %param.10), kind=kOutput, calls=%fused_computation.9 | convolution fusion | flops 4039114752 | bytes 13500416 | tf_op jit(solution)/shard_map/dot_general | solution.py:39
  173.5 19.5 %convolution_convert_fusion = bf16[640,4096]{1,0:T(8,128)(2,1)} fusion(bf16[384,4096]{1,0:T(8,128)(2,1)} %collective-permute-done.2, bf16[384,4096]{1,0:T(8,128)(2,1)} %param.11, f32[640,768]{1,0:T(8,128)S(1)} %fusion.5, bf16[640,4096]{1,0:T(8,128)(2,1)} %reshape.41, bf16[4096,384]{1,0:T(8,128)(2,1)} %collective-permute-done, bf16[4096,384]{1,0:T(8,128)(2,1)} %param.9), kind=kOutput, calls=%fused_computation.3 | convolution fusion | flops 8083800064 | bytes 25034752 | tf_op jit(solution)/shard_map/dot_general | solution.py:41
  193.0 7.6 %reshape.42 = bf16[32,20,4096]{2,1,0:T(8,128)(2,1)} reshape(bf16[640,4096]{1,0:T(8,128)(2,1)} %convolution_convert_fusion) | data formatting | bytes 10485760 | tf_op jit(solution)/shard_map/reshape | solution.py:42
  200.6 8.1 %all-to-all-start.1 = ((bf16[32,20,4096]{2,1,0:T(8,128)(2,1)}), bf16[32,20,4096]{2,1,0:T(8,128)(2,1)}, u32[]{:S(2)}, u32[]{:S(2)}) async-start(bf16[32,20,4096]{2,1,0:T(8,128)(2,1)} %reshape.42), calls=%async_computation.1 | async-start | bytes 12582912 | tf_op jit(solution)/shard_map/all_to_all | solution.py:43
  208.7 0.1 reshape.46
  208.9 135.1 %all-to-all-done.1 = bf16[32,20,4096]{2,1,0:T(8,128)(2,1)} async-done(((bf16[32,20,4096]{2,1,0:T(8,128)(2,1)}), bf16[32,20,4096]{2,1,0:T(8,128)(2,1)}, u32[]{:S(2)}, u32[]{:S(2)}) %all-to-all-start.1) | async-done | bytes 5242912 | tf_op jit(solution)/shard_map/all_to_all | solution.py:43
  344.1 7.8 %reshape.43 = bf16[640,4096]{1,0:T(8,128)(2,1)} reshape(bf16[32,20,4096]{2,1,0:T(8,128)(2,1)} %all-to-all-done.1) | data formatting | bytes 10485760 | tf_op jit(solution)/shard_map/reshape | solution.py:44
  351.9 11.8 %gather_fusion = bf16[512,4096]{1,0:T(8,128)(2,1)} fusion(bf16[640,4096]{1,0:T(8,128)(2,1)} %reshape.43, s32[1024]{0:T(1024)S(1)} %pad_clamp_fusion), kind=kCustom, calls=%fused_computation | custom fusion | bytes 8390656 | tf_op jit(solution)/shard_map/gather | solution.py:45
  363.7 6.5 %fusion = bf16[64,4096]{1,0:T(8,128)(2,1)} fusion(bf16[512,4096]{1,0:T(8,128)(2,1)} %gather_fusion, f32[64,8]{1,0:T(8,128)S(1)} %copy.21), kind=kLoop, calls=%fused_computation.2 | loop fusion | flops 6029312 | bytes 4720640 | tf_op jit(solution)/shard_map/reduce_sum | solution.py:46
  (19 shorter events, 0.6 us)
Async XLA Ops:
  0.0 4.0 %copy-start = (bf16[64,4096]{1,0:T(8,128)(2,1)S(1)}, bf16[64,4096]{1,0:T(8,128)(2,1)}, u32[]{:S(2)}) copy-start(bf16[64,4096]{1,0:T(8,128)(2,1)} %param.6) | copy-start | bytes 1572868
  15.5 141.6 %all-to-all-start = ((bf16[32,20,4096]{2,1,0:T(8,128)(2,1)}), bf16[32,20,4096]{2,1,0:T(8,128)(2,1)}, u32[]{:S(2)}, u32[]{:S(2)}) async-start(bf16[32,20,4096]{2,1,0:T(8,128)(2,1)} %reshape.40), calls=%async_computation | async-start | bytes 12582912 | tf_op jit(solution)/shard_map/all_to_all | solution.py:36
  21.6 143.3 %collective-permute-start.1 = (bf16[4096,384]{1,0:T(8,128)(2,1)}, bf16[4096,384]{1,0:T(8,128)(2,1)}, u32[]{:S(2)}, u32[]{:S(2)}) collective-permute-start(bf16[4096,384]{1,0:T(8,128)(2,1)} %param.10), channel_id=1, source_target_pairs={{0,1},{1,0},{2,3},{3,2},{4,5},{5,4},{6,7},{7,6},{8,9},{9,8},{10,11... | collective-permute-start | bytes 9437192 | tf_op jit(solution)/shard_map/ppermute | solution.py:10
  21.7 151.7 %collective-permute-start = (bf16[4096,384]{1,0:T(8,128)(2,1)}, bf16[4096,384]{1,0:T(8,128)(2,1)}, u32[]{:S(2)}, u32[]{:S(2)}) collective-permute-start(bf16[4096,384]{1,0:T(8,128)(2,1)} %param.9), channel_id=1, source_target_pairs={{0,1},{1,0},{2,3},{3,2},{4,5},{5,4},{6,7},{7,6},{8,9},{9,8},{10,11... | collective-permute-start | bytes 9437192 | tf_op jit(solution)/shard_map/ppermute | solution.py:10
  22.1 151.4 %collective-permute-start.2 = (bf16[384,4096]{1,0:T(8,128)(2,1)}, bf16[384,4096]{1,0:T(8,128)(2,1)}, u32[]{:S(2)}, u32[]{:S(2)}) collective-permute-start(bf16[384,4096]{1,0:T(8,128)(2,1)} %param.11), channel_id=1, source_target_pairs={{0,1},{1,0},{2,3},{3,2},{4,5},{5,4},{6,7},{7,6},{8,9},{9,8},{10,11... | collective-permute-start | bytes 9437192 | tf_op jit(solution)/shard_map/ppermute | solution.py:10
  200.6 8.3 %copy-start.2 = (f32[64,8]{0,1:T(8,128)S(1)}, f32[64,8]{0,1:T(8,128)}, u32[]{:S(2)}) copy-start(f32[64,8]{0,1:T(8,128)} %param.8) | copy-start | bytes 6148
  200.6 143.5 %all-to-all-start.1 = ((bf16[32,20,4096]{2,1,0:T(8,128)(2,1)}), bf16[32,20,4096]{2,1,0:T(8,128)(2,1)}, u32[]{:S(2)}, u32[]{:S(2)}) async-start(bf16[32,20,4096]{2,1,0:T(8,128)(2,1)} %reshape.42), calls=%async_computation.1 | async-start | bytes 12582912 | tf_op jit(solution)/shard_map/all_to_all | solution.py:43
  351.9 18.2 %copy-start.1 = (bf16[64,4096]{1,0:T(8,128)(2,1)S(1)}, bf16[64,4096]{1,0:T(8,128)(2,1)}, u32[]{:S(2)}) copy-start(bf16[64,4096]{1,0:T(8,128)(2,1)} %param.6) | copy-start | bytes 1572868
where the time goes:
time: 377 us; the launch traced here: 370 us
  waiting for transfers between devices  270 us (72%)
  local copies, waits for them, and re-layouts  44.4 us (12%)
  matrix products  31.9 us (8%)
  starting transfers between devices  14.8 us (4%)
  other arithmetic  8.92 us (2%)
    all_to_all x1, waiting for transfers between devices, per_device(): lax.all_to_all(processed, ('node', 'local'), split_axis=0, concat_axis=0,...  135 us
    all_to_all x1, waiting for transfers between devices, per_device(): lax.all_to_all(outgoing, ('node', 'local'), split_axis=0, concat_axis=0,...  135 us
    dot_general x1, matrix products, per_device(): jnp.dot(hidden, full_down, preferred_element_type=jnp.float32)  19.5 us
    gather x1, local copies, waits for them, and re-layouts, per_device(): chosen = results[slot_index]  11.8 us
    dot_general x1, matrix products, per_device(): upper = jnp.dot(rows, full_up, preferred_element_type=jnp.float32)  8.6 us
    all_to_all x1, starting transfers between devices, per_device(): lax.all_to_all(processed, ('node', 'local'), split_axis=0, concat_axis=0,...  8.06 us
    reshape x1, local copies, waits for them, and re-layouts, per_device(): rows = block.reshape(-1, width)  7.84 us
    reshape x1, local copies, waits for them, and re-layouts, per_device(): results = returned.reshape(experts * capacity, width)  7.84 us
  transfers between devices with their start and end apart: 5, of which 2 were waited for; matrix products, arithmetic and copies ran while one was open for 5% of the time, Pallas kernels for 0%

commit v1 on v0

--- a/solution.py
+++ b/solution.py
@@ -1,7 +1,13 @@
+import functools
+
 import jax
 import jax.numpy as jnp
 from jax import lax
+from jax.experimental import pallas as pl
+from jax.experimental.pallas import tpu as pltpu
 from jax.sharding import PartitionSpec as P
+
+MESH = pl.DeviceIdType.MESH
 
 
 def partner_2(value, axis, bit):
@@ -10,7 +16,7 @@
     return lax.ppermute(value, axis, pairs)
 
 
-def per_device(tokens, expert_ids, gate_weights, w_gate, w_up, w_down):
+def by_slots(tokens, expert_ids, gate_weights, w_gate, w_up, w_down):
     node_count = lax.axis_size("node")
     local_count = lax.axis_size("local")
     devices = node_count * local_count
@@ -47,6 +53,270 @@
     return mixed.astype(jnp.bfloat16)
 
 
+LANES = 128
+
+
+def layer_kernel(
+    nodes, columns, width, hidden_half,
+    rows_ref, gate_ref, up_ref, down_ref, out_ref,
+    taken, first, second, sums, firsts, seconds, finals, acts, hidden, totals,
+    load_sem, swap_send, swap_recv, col_send, col_recv, own_send, own_recv, far_send, far_recv,
+    one_send, one_recv, two_send, two_recv, end_send, end_recv,
+):
+    part, node, local = lax.axis_index("parts"), lax.axis_index("node"), lax.axis_index("local")
+    column, half = local // 2, lax.rem(local, 2)
+    high, low = node // 2, lax.rem(node, 2)
+    count = rows_ref.shape[0]
+    split = width // 2
+    wide = rows_ref.shape[1]
+
+    def at(node_index, local_index):
+        return (part, node_index, local_index)
+
+    sides = (at(high * 2 + 1 - low, local), at((1 - high) * 2 + low, local))
+    twin = at(node, column * 2 + 1 - half)
+
+    def along(step):
+        low_bit = lax.rem(column, 2)
+        if step & 1:
+            low_bit = 1 - low_bit
+        rest, bit = column // 2, 1
+        place = low_bit
+        while (1 << bit) < columns:
+            value = lax.rem(rest, 2)
+            if step >> bit & 1:
+                value = 1 - value
+            place = place + value * (1 << bit)
+            rest, bit = rest // 2, bit + 1
+        return at(node, place * 2 + half)
+
+    peers = [along(step) for step in range(1, columns)]
+    barrier = pltpu.get_barrier_semaphore()
+    for peer in (*sides, twin, *peers):
+        pl.semaphore_signal(barrier, inc=1, device_id=peer, device_id_type=MESH)
+    pl.semaphore_wait(barrier, 3 + len(peers))
+
+    def send(source, target, send_sem, recv_sem, peer):
+        return pltpu.make_async_remote_copy(
+            src_ref=source, dst_ref=target, send_sem=send_sem, recv_sem=recv_sem,
+            device_id=peer, device_id_type=MESH,
+        )
+
+    everything = []
+
+    def start(copy):
+        copy.start()
+        everything.append(copy)
+        return copy
+
+    def block(step, slot):
+        return taken.at[step, pl.ds(slot * count, count)]
+
+    def columns_of(side):
+        return pl.ds(0, split) if side == 0 else pl.ds(split, wide - split)
+
+    near = (
+        (gate_ref, first, 0, False), (up_ref, first, 1, False), (down_ref, second, 0, True),
+    )
+    loads, swaps = [], []
+
+    def spot(target, index, by_rows, other):
+        place = pl.ds((index + other) * hidden_half, hidden_half)
+        return target.at[place] if by_rows else target.at[:, place]
+
+    own = [start(send(rows_ref, block(0, side + 1), own_send.at[0, side], own_recv.at[0, side], sides[side])) for side in (0, 1)]
+    spread = [start(send(rows_ref, block(step, 0), col_send.at[step], col_recv.at[step], peers[step - 1])) for step in range(1, columns)]
+    for number, (source, target, index, by_rows) in enumerate(near):
+        swaps.append(start(send(source, spot(target, index, by_rows, 1 if by_rows else 2), swap_send.at[number], swap_recv.at[number], twin)))
+    for number, (source, target, index, by_rows) in enumerate(near):
+        loads.append(pltpu.make_async_copy(source, spot(target, index, by_rows, 0), load_sem.at[number]))
+    loads.append(pltpu.make_async_copy(rows_ref, block(0, 0), load_sem.at[len(near)]))
+    for copy in loads:
+        copy.start()
+
+    nears, fars = [own], []
+
+    def pass_on(step):
+        moved = []
+        for side in (0, 1):
+            nears[step][side].wait_recv()
+            piece = taken.at[step, pl.ds((side + 1) * count, count), columns_of(side)]
+            target = taken.at[step, pl.ds(3 * count, count), columns_of(side)]
+            moved.append(start(send(piece, target, far_send.at[step, side], far_recv.at[step, side], sides[1 - side])))
+        fars.append(moved)
+
+    def share_out(step):
+        spread[step - 1].wait_recv()
+        nears.append([
+            start(send(block(step, 0), block(step, side + 1), own_send.at[step, side], own_recv.at[step, side], sides[side]))
+            for side in (0, 1)
+        ])
+
+    def compute(step):
+        for copy in fars[step]:
+            copy.wait_recv()
+        expert = node * columns + column
+        table = taken[step, :, pl.ds(width, LANES)].astype(jnp.float32)
+        lane = lax.broadcasted_iota(jnp.int32, table.shape, 1)
+        chosen = (lane == expert) | (lane == expert + nodes * columns) | (lane == expert + 2 * nodes * columns)
+        share = jnp.sum(jnp.where(chosen, table, 0.0), axis=1, keepdims=True)
+        tile = 2 * LANES
+
+        def into(index, carry):
+            place = pl.ds(pl.multiple_of(index * tile, tile), tile)
+            acts[:, place] = jnp.dot(taken[step, :, pl.ds(0, width)], first[:, place], preferred_element_type=jnp.float32)
+            return carry
+
+        lax.fori_loop(0, acts.shape[1] // tile, into, 0)
+        for other in (0, 1):
+            gate = acts[:, pl.ds(2 * other * hidden_half, hidden_half)]
+            upper = acts[:, pl.ds((2 * other + 1) * hidden_half, hidden_half)]
+            hidden[:, pl.ds(other * hidden_half, hidden_half)] = (gate / (1.0 + jnp.exp(-gate)) * upper).astype(jnp.bfloat16)
+        share_wide = jnp.broadcast_to(share, (4 * count, tile))
+        for side in (0, 1):
+            def out_of(index, carry, side=side):
+                place = pl.ds(pl.multiple_of(index * tile, tile), tile)
+                source = pl.ds(pl.multiple_of(side * split + index * tile, tile), tile)
+                result = jnp.dot(hidden[...], second[:, source], preferred_element_type=jnp.float32)
+                result = (result * share_wide).astype(jnp.bfloat16)
+                order = (0, 2, 1, 3) if side == 0 else (0, 1, 2, 3)
+                for slot in range(4):
+                    sums[side, step, pl.ds(order[slot] * count, count), place] = result[slot * count:(slot + 1) * count]
+                return carry
+
+            lax.fori_loop(0, split // tile, out_of, 0)
+
+    ones, twos, ends = {}, {}, {}
+
+    def reduce_one(step):
+        ones[step] = [
+            start(send(sums.at[side, step, pl.ds(2 * count, 2 * count)], firsts.at[side, step], one_send.at[step, side], one_recv.at[step, side], sides[side]))
+            for side in (0, 1)
+        ]
+
+    def add(side, step, start_row, rows, source):
+        def body(index, carry):
+            place = pl.ds(start_row + index * 16, 16)
+            other = pl.ds(index * 16, 16)
+            total = sums[side, step, place].astype(jnp.float32) + source[side, step, other].astype(jnp.float32)
+            sums[side, step, place] = total.astype(jnp.bfloat16)
+            return carry
+
+        lax.fori_loop(0, rows // 16, body, 0)
+
+    def reduce_two(step):
+        twos[step] = []
+        for side in (0, 1):
+            ones[step][side].wait_recv()
+            add(side, step, 0, 2 * count, firsts)
+            twos[step].append(start(send(sums.at[side, step, pl.ds(count, count)], seconds.at[side, step], two_send.at[step, side], two_recv.at[step, side], sides[1 - side])))
+
+    def reduce_end(step):
+        for side in (0, 1):
+            twos[step][side].wait_recv()
+            add(side, step, 0, count, seconds)
+        if step:
+            ends[step] = [
+                start(send(sums.at[side, step, pl.ds(0, count)], finals.at[side, step - 1], end_send.at[step, side], end_recv.at[step, side], peers[step - 1]))
+                for side in (0, 1)
+            ]
+
+    pass_on(0)
+    if columns > 1:
+        share_out(1)
+    for copy in swaps:
+        copy.wait_recv()
+    for copy in loads:
+        copy.wait()
+    for step in range(columns):
+        if step >= 1:
+            pass_on(step)
+            if step + 1 < columns:
+                share_out(step + 1)
+        if step >= 3:
+            reduce_end(step - 3)
+        if step >= 2:
+            reduce_two(step - 2)
+        compute(step)
+        reduce_one(step)
+    for step in range(max(0, columns - 3), columns + 2):
+        if step < columns and step >= columns - 2 and step >= 0:
+            reduce_two(step)
+        if step - 1 >= max(0, columns - 3) and step - 1 < columns:
+            reduce_end(step - 1)
+    for step in range(1, columns):
+        for copy in ends[step]:
+            copy.wait_recv()
+    for side in (0, 1):
+        def body(index, carry, side=side):
+            place = pl.ds(index * 16, 16)
+            total = sums[side, 0, place].astype(jnp.float32)
+            for step in range(1, columns):
+                total = total + finals[side, step - 1, place].astype(jnp.float32)
+            totals[place, pl.ds(side * split, split)] = total.astype(jnp.bfloat16)
+            return carry
+
+        lax.fori_loop(0, count // 16, body, 0)
+    result = pltpu.make_async_copy(totals, out_ref, load_sem.at[0])
+    result.start()
+    for copy in everything:
+        copy.wait_send()
+    result.wait()
+
+
+def by_rows(tokens, expert_ids, gate_weights, w_gate, w_up, w_down):
+    nodes, columns = lax.axis_size("node"), lax.axis_size("local") // 2
+    experts = nodes * columns
+    count, width = tokens.shape
+    hidden_half = w_gate.shape[1]
+    hits = expert_ids[:, :, None] == jnp.arange(experts, dtype=jnp.int32)[None, None, :]
+    table = jnp.sum(jnp.where(hits, gate_weights[:, :, None], 0.0), axis=1)
+    pieces = []
+    for _ in range(3):
+        piece = lax.reduce_precision(table, 8, 7)
+        pieces.append(piece.astype(jnp.bfloat16))
+        table = table - piece
+    pieces = jnp.concatenate(pieces, axis=1)
+    pieces = jnp.pad(pieces, ((0, 0), (0, LANES - pieces.shape[1])))
+    rows = jnp.concatenate([tokens, pieces], axis=1)
+    wide = rows.shape[1]
+    split = width // 2
+    dma = pltpu.SemaphoreType.DMA
+    bf16 = jnp.bfloat16
+    scratch = [
+        pltpu.VMEM((columns, 4 * count, wide), bf16),
+        pltpu.VMEM((width, 4 * hidden_half), bf16),
+        pltpu.VMEM((2 * hidden_half, width), bf16),
+        pltpu.VMEM((2, columns, 4 * count, split), bf16),
+        pltpu.VMEM((2, columns, 2 * count, split), bf16),
+        pltpu.VMEM((2, columns, count, split), bf16),
+        pltpu.VMEM((2, columns - 1, count, split), bf16),
+        pltpu.VMEM((4 * count, 4 * hidden_half), jnp.float32),
+        pltpu.VMEM((4 * count, 2 * hidden_half), bf16),
+        pltpu.VMEM((count, width), bf16),
+        dma((4,)), dma((3,)), dma((3,)), dma((columns,)), dma((columns,)),
+    ] + [dma((columns, 2)) for _ in range(10)]
+    flops = 12 * experts * count * width * hidden_half
+    return pl.pallas_call(
+        functools.partial(layer_kernel, nodes, columns, width, hidden_half),
+        name="moe_layer",
+        out_shape=jax.ShapeDtypeStruct((count, width), bf16),
+        in_specs=[pl.BlockSpec(memory_space=pl.ANY)] * 4,
+        out_specs=pl.BlockSpec(memory_space=pl.ANY),
+        scratch_shapes=scratch,
+        cost_estimate=pl.CostEstimate(flops=flops, bytes_accessed=w_gate.size * 12, transcendentals=0),
+        compiler_params=pltpu.CompilerParams(collective_id=0, has_side_effects=True, vmem_limit_bytes=60 << 20),
+    )(rows, w_gate, w_up, w_down)
+
+
+def per_device(tokens, expert_ids, *rest):
+    nodes, columns = lax.axis_size("node"), lax.axis_size("local") // 2
+    dense_enough = nodes * columns <= 2 * expert_ids.shape[1]
+    if nodes == 4 and columns & (columns - 1) == 0 and dense_enough:
+        return by_rows(tokens, expert_ids, *rest)
+    return by_slots(tokens, expert_ids, *rest)
+
+
 def solution(mesh):
     placed = (
         P(("parts", "node", "local"), None),

time: 377 us -> 190 us (0.50); the launches traced: 370 us -> 190 us
  waiting for transfers between devices: 270 us -> 0 us
  Pallas kernels: 0 us -> 185 us
  local copies, waits for them, and re-layouts: 44.4 us -> 2.03 us
  matrix products: 31.9 us -> 0 us
  starting transfers between devices: 14.8 us -> 0 us
  other arithmetic: 8.92 us -> 2.69 us
    all_to_all x2 -> x0, waiting for transfers between devices: 270 us -> none  [the longest x1 135 us: per_device(): lax.all_to_all(processed, ('node', 'local'), split_axis=0, concat_axis=0,...]
    pallas_call x0 -> x1, Pallas kernels: none -> 185 us  [by_rows(): pl.pallas_call(functools.partial(layer_kernel, nodes, columns, width, hid...]
    dot_general x3 -> x0, matrix products: 31.9 us -> none  [the longest x1 19.5 us: per_device(): jnp.dot(hidden, full_down, preferred_element_type=jnp.float32)]
    reshape x4 -> x0, local copies, waits for them, and re-layouts: 30.9 us -> none  [the longest x1 7.84 us: per_device(): rows = block.reshape(-1, width)]
    all_to_all x2 -> x0, starting transfers between devices: 14.1 us -> none  [the longest x1 8.06 us: per_device(): lax.all_to_all(processed, ('node', 'local'), split_axis=0, concat_axis=0,...]
    gather x1 -> x0, local copies, waits for them, and re-layouts: 11.8 us -> none  [per_device(): chosen = results[slot_index]]
    reduce_sum x2 -> x1, other arithmetic: 6.56 us -> 0.72 us  [by_rows(): table = jnp.sum(jnp.where(hits, gate_weights[:, :, None], 0.0), axis=1)]
  transfers between devices with their start and end apart: 5 -> 0, of which waited for: 2 -> 0; matrix products, arithmetic and copies ran while one was open for 5% -> 0% of each run, Pallas kernels for 0% -> 0%
where the time goes in v1:
time: 190 us
  Pallas kernels  185 us (97%)
  other arithmetic  2.69 us (1%)
  local copies, waits for them, and re-layouts  2.03 us (1%)
    pallas_call x1, Pallas kernels, by_rows(): pl.pallas_call(functools.partial(layer_kernel, nodes, columns, width, hid...  185 us

profile of v1, /device:TPU:10, one launch (start us, length us, event | category | flops | bytes accessed | tf_op | source)
XLA Modules:
  0.0 190.1 jit_solution(1981390653954879868)
XLA Ops:
  0.0 0.7 select_reduce_fusion
  0.7 0.1 copy.12
  0.8 0.1 copy.11
  0.9 0.1 fusion.6
  1.0 1.9 pad_maximum_fusion.rows_ref
  2.9 185.4 %moe_layer.1 = bf16[64,4096]{1,0:T(8,128)(2,1)} custom-call(bf16[64,4224]{1,0:T(8,128)(2,1)} %pad_maximum_fusion.rows_ref, bf16[4096,384]{1,0:T(8,128)(2,1)} %gate_ref.1, bf16[4096,384]{1,0:T(8,128)(2,1)} %up_ref.1, bf16[384,4096]{1,0:T(8,128)(2,1)} %down_ref.1), custom_call_target="tpu_custom_call" | custom-call | flops 19327352832 | bytes 18874368 | tf_op jit(solution)/shard_map/moe_layer/pallas_call | solution.py:300
  188.2 1.9 copy.15
  (2 shorter events, 0.0 us)

commit v2 on v1

--- a/solution.py
+++ b/solution.py
@@ -221,29 +221,44 @@
                 for side in (0, 1)
             ]
 
+    last = columns - 1
     pass_on(0)
-    if columns > 1:
+    if last:
         share_out(1)
     for copy in swaps:
         copy.wait_recv()
     for copy in loads:
         copy.wait()
-    for step in range(columns):
-        if step >= 1:
-            pass_on(step)
-            if step + 1 < columns:
-                share_out(step + 1)
-        if step >= 3:
-            reduce_end(step - 3)
-        if step >= 2:
-            reduce_two(step - 2)
+    if last:
+        pass_on(1)
+    compute(0)
+    for step in range(1, columns):
+        if step >= 2 and step < last:
+            share_out(step + 1)
+            reduce_two(step - 1)
+        elif step == 1 and step < last:
+            share_out(2)
         compute(step)
+        if step == 1 and step < last:
+            reduce_one(1)
+            pass_on(2)
+            continue
+        if step < last:
+            pass_on(step + 1)
         reduce_one(step)
-    for step in range(max(0, columns - 3), columns + 2):
-        if step < columns and step >= columns - 2 and step >= 0:
-            reduce_two(step)
-        if step - 1 >= max(0, columns - 3) and step - 1 < columns:
+        if step < last:
             reduce_end(step - 1)
+    if last >= 2:
+        reduce_two(last - 1)
+    if last:
+        reduce_two(last)
+    reduce_one(0)
+    if last >= 2:
+        reduce_end(last - 1)
+    if last:
+        reduce_end(last)
+    reduce_two(0)
+    reduce_end(0)
     for step in range(1, columns):
         for copy in ends[step]:
             copy.wait_recv()

time: 190 us -> 175 us (0.921)
  Pallas kernels: 185 us -> 170 us
    pallas_call x1, Pallas kernels: 185 us -> 170 us  [by_rows(): pl.pallas_call(functools.partial(layer_kernel, nodes, columns, width, hid...]
where the time goes in v2:
time: 175 us
  Pallas kernels  170 us (97%)
  other arithmetic  2.69 us (2%)
  local copies, waits for them, and re-layouts  2.03 us (1%)
    pallas_call x1, Pallas kernels, by_rows(): pl.pallas_call(functools.partial(layer_kernel, nodes, columns, width, hid...  170 us

profile of v2, /device:TPU:10, one launch (start us, length us, event | category | flops | bytes accessed | tf_op | source)
XLA Modules:
  0.0 175.0 jit_solution(15710091246510338704)
XLA Ops:
  0.0 0.7 select_reduce_fusion
  0.7 0.1 copy.12
  0.8 0.1 copy.11
  0.9 0.1 fusion.6
  1.0 1.9 %pad_maximum_fusion.rows_ref = bf16[64,4224]{1,0:T(8,128)(2,1)} fusion(bf16[64,128]{1,0:T(8,128)(2,1)S(1)} %fusion.6, bf16[64,4096]{1,0:T(8,128)(2,1)} %param.6), kind=kLoop, calls=%fused_computation | loop fusion | flops 1081344 | bytes 1081344 | tf_op jit(solution)/shard_map/concatenate | solution.py:296
  2.9 170.3 %moe_layer.1 = bf16[64,4096]{1,0:T(8,128)(2,1)} custom-call(bf16[64,4224]{1,0:T(8,128)(2,1)} %pad_maximum_fusion.rows_ref, bf16[4096,384]{1,0:T(8,128)(2,1)} %gate_ref.1, bf16[4096,384]{1,0:T(8,128)(2,1)} %up_ref.1, bf16[384,4096]{1,0:T(8,128)(2,1)} %down_ref.1), custom_call_target="tpu_custom_call" | custom-call | flops 19327352832 | bytes 18874368 | tf_op jit(solution)/shard_map/moe_layer/pallas_call | solution.py:315
  173.2 1.9 %copy.15 = bf16[64,4096]{1,0:T(8,128)(2,1)} copy(bf16[64,4096]{1,0:T(8,128)(2,1)} %moe_layer.1) | data formatting | bytes 1048576
  (2 shorter events, 0.0 us)

commit v3 on v2

--- a/solution.py
+++ b/solution.py
@@ -57,11 +57,12 @@
 
 
 def layer_kernel(
-    nodes, columns, width, hidden_half,
+    nodes, columns, width, hidden_half, extra,
     rows_ref, gate_ref, up_ref, down_ref, out_ref,
     taken, first, second, sums, firsts, seconds, finals, acts, hidden, totals,
     load_sem, swap_send, swap_recv, col_send, col_recv, own_send, own_recv, far_send, far_recv,
     one_send, one_recv, two_send, two_recv, end_send, end_recv,
+    early_send, early_recv, late_send, late_recv, lates,
 ):
     part, node, local = lax.axis_index("parts"), lax.axis_index("node"), lax.axis_index("local")
     column, half = local // 2, lax.rem(local, 2)
@@ -69,6 +70,9 @@
     count = rows_ref.shape[0]
     split = width // 2
     wide = rows_ref.shape[1]
+    middle = LANES + (width - extra) // 2
+    body_end = wide - extra
+    kept = split - extra // 2
 
     def at(node_index, local_index):
         return (part, node_index, local_index)
@@ -112,8 +116,9 @@
     def block(step, slot):
         return taken.at[step, pl.ds(slot * count, count)]
 
-    def columns_of(side):
-        return pl.ds(0, split) if side == 0 else pl.ds(split, wide - split)
+    def columns_of(step, side):
+        end = body_end if step else wide
+        return pl.ds(0, middle) if side == 0 else pl.ds(middle, end - middle)
 
     near = (
         (gate_ref, first, 0, False), (up_ref, first, 1, False), (down_ref, second, 0, True),
@@ -125,7 +130,7 @@
         return target.at[place] if by_rows else target.at[:, place]
 
     own = [start(send(rows_ref, block(0, side + 1), own_send.at[0, side], own_recv.at[0, side], sides[side])) for side in (0, 1)]
-    spread = [start(send(rows_ref, block(step, 0), col_send.at[step], col_recv.at[step], peers[step - 1])) for step in range(1, columns)]
+    spread = [start(send(rows_ref.at[:, pl.ds(0, body_end)], block(step, 0).at[:, pl.ds(0, body_end)], col_send.at[step], col_recv.at[step], peers[step - 1])) for step in range(1, columns)]
     for number, (source, target, index, by_rows) in enumerate(near):
         swaps.append(start(send(source, spot(target, index, by_rows, 1 if by_rows else 2), swap_send.at[number], swap_recv.at[number], twin)))
     for number, (source, target, index, by_rows) in enumerate(near):
@@ -140,23 +145,34 @@
         moved = []
         for side in (0, 1):
             nears[step][side].wait_recv()
-            piece = taken.at[step, pl.ds((side + 1) * count, count), columns_of(side)]
-            target = taken.at[step, pl.ds(3 * count, count), columns_of(side)]
+            piece = taken.at[step, pl.ds((side + 1) * count, count), columns_of(step, side)]
+            target = taken.at[step, pl.ds(3 * count, count), columns_of(step, side)]
             moved.append(start(send(piece, target, far_send.at[step, side], far_recv.at[step, side], sides[1 - side])))
         fars.append(moved)
 
     def share_out(step):
         spread[step - 1].wait_recv()
         nears.append([
-            start(send(block(step, 0), block(step, side + 1), own_send.at[step, side], own_recv.at[step, side], sides[side]))
+            start(send(block(step, 0).at[:, pl.ds(0, body_end)], block(step, side + 1).at[:, pl.ds(0, body_end)], own_send.at[step, side], own_recv.at[step, side], sides[side]))
             for side in (0, 1)
         ])
 
+    earlies, late = {}, {}
+
+    def spread_extra():
+        for copy in fars[0]:
+            copy.wait_recv()
+        place = pl.ds(body_end, extra)
+        for step in range(1, columns):
+            earlies[step] = start(send(taken.at[0, :, place], taken.at[step, :, place], early_send.at[step], early_recv.at[step], peers[step - 1]))
+
     def compute(step):
-        for copy in fars[step]:
-            copy.wait_recv()
+        if step:
+            for copy in fars[step]:
+                copy.wait_recv()
+            earlies[step].wait_recv()
         expert = node * columns + column
-        table = taken[step, :, pl.ds(width, LANES)].astype(jnp.float32)
+        table = taken[step, :, pl.ds(0, LANES)].astype(jnp.float32)
         lane = lax.broadcasted_iota(jnp.int32, table.shape, 1)
         chosen = (lane == expert) | (lane == expert + nodes * columns) | (lane == expert + 2 * nodes * columns)
         share = jnp.sum(jnp.where(chosen, table, 0.0), axis=1, keepdims=True)
@@ -164,7 +180,7 @@
 
         def into(index, carry):
             place = pl.ds(pl.multiple_of(index * tile, tile), tile)
-            acts[:, place] = jnp.dot(taken[step, :, pl.ds(0, width)], first[:, place], preferred_element_type=jnp.float32)
+            acts[:, place] = jnp.dot(taken[step, :, pl.ds(LANES, width)], first[:, place], preferred_element_type=jnp.float32)
             return carry
 
         lax.fori_loop(0, acts.shape[1] // tile, into, 0)
@@ -185,12 +201,37 @@
                 return carry
 
             lax.fori_loop(0, split // tile, out_of, 0)
+        if step:
+            place = pl.ds(kept, split - kept)
+            late[step] = [
+                start(send(sums.at[side, step, :, place], lates.at[side, step - 1], late_send.at[step, side], late_recv.at[step, side], peers[step - 1]))
+                for side in (0, 1)
+            ]
+
+    def span(step):
+        return pl.ds(0, kept if step else split)
+
+    def gather_late():
+        for step in range(1, columns):
+            for copy in late[step]:
+                copy.wait_recv()
+        place = pl.ds(kept, split - kept)
+        for side in (0, 1):
+            def body(index, carry, side=side):
+                rows = pl.ds(index * 16, 16)
+                total = sums[side, 0, rows, place].astype(jnp.float32)
+                for step in range(1, columns):
+                    total = total + lates[side, step - 1, rows].astype(jnp.float32)
+                sums[side, 0, rows, place] = total.astype(jnp.bfloat16)
+                return carry
+
+            lax.fori_loop(0, 4 * count // 16, body, 0)
 
     ones, twos, ends = {}, {}, {}
 
     def reduce_one(step):
         ones[step] = [
-            start(send(sums.at[side, step, pl.ds(2 * count, 2 * count)], firsts.at[side, step], one_send.at[step, side], one_recv.at[step, side], sides[side]))
+            start(send(sums.at[side, step, pl.ds(2 * count, 2 * count), span(step)], firsts.at[side, step, :, span(step)], one_send.at[step, side], one_recv.at[step, side], sides[side]))
             for side in (0, 1)
         ]
 
@@ -198,8 +239,9 @@
         def body(index, carry):
             place = pl.ds(start_row + index * 16, 16)
             other = pl.ds(index * 16, 16)
-            total = sums[side, step, place].astype(jnp.float32) + source[side, step, other].astype(jnp.float32)
-            sums[side, step, place] = total.astype(jnp.bfloat16)
+            lanes = span(step)
+            total = sums[side, step, place, lanes].astype(jnp.float32) + source[side, step, other, lanes].astype(jnp.float32)
+            sums[side, step, place, lanes] = total.astype(jnp.bfloat16)
             return carry
 
         lax.fori_loop(0, rows // 16, body, 0)
@@ -209,7 +251,7 @@
         for side in (0, 1):
             ones[step][side].wait_recv()
             add(side, step, 0, 2 * count, firsts)
-            twos[step].append(start(send(sums.at[side, step, pl.ds(count, count)], seconds.at[side, step], two_send.at[step, side], two_recv.at[step, side], sides[1 - side])))
+            twos[step].append(start(send(sums.at[side, step, pl.ds(count, count), span(step)], seconds.at[side, step, :, span(step)], two_send.at[step, side], two_recv.at[step, side], sides[1 - side])))
 
     def reduce_end(step):
         for side in (0, 1):
@@ -217,7 +259,7 @@
             add(side, step, 0, count, seconds)
         if step:
             ends[step] = [
-                start(send(sums.at[side, step, pl.ds(0, count)], finals.at[side, step - 1], end_send.at[step, side], end_recv.at[step, side], peers[step - 1]))
+                start(send(sums.at[side, step, pl.ds(0, count), span(step)], finals.at[side, step - 1], end_send.at[step, side], end_recv.at[step, side], peers[step - 1]))
                 for side in (0, 1)
             ]
 
@@ -229,6 +271,7 @@
         copy.wait_recv()
     for copy in loads:
         copy.wait()
+    spread_extra()
     if last:
         pass_on(1)
     compute(0)
@@ -252,6 +295,7 @@
         reduce_two(last - 1)
     if last:
         reduce_two(last)
+    gather_late()
     reduce_one(0)
     if last >= 2:
         reduce_end(last - 1)
@@ -265,10 +309,11 @@
     for side in (0, 1):
         def body(index, carry, side=side):
             place = pl.ds(index * 16, 16)
-            total = sums[side, 0, place].astype(jnp.float32)
+            total = sums[side, 0, place, pl.ds(0, kept)].astype(jnp.float32)
             for step in range(1, columns):
                 total = total + finals[side, step - 1, place].astype(jnp.float32)
-            totals[place, pl.ds(side * split, split)] = total.astype(jnp.bfloat16)
+            totals[place, pl.ds(side * split, kept)] = total.astype(jnp.bfloat16)
+            totals[place, pl.ds(side * split + kept, split - kept)] = sums[side, 0, place, pl.ds(kept, split - kept)]
             return carry
 
         lax.fori_loop(0, count // 16, body, 0)
@@ -293,9 +338,11 @@
         table = table - piece
     pieces = jnp.concatenate(pieces, axis=1)
     pieces = jnp.pad(pieces, ((0, 0), (0, LANES - pieces.shape[1])))
-    rows = jnp.concatenate([tokens, pieces], axis=1)
+    rows = jnp.concatenate([pieces, tokens], axis=1)
     wide = rows.shape[1]
     split = width // 2
+    extra = width // 8
+    kept = split - extra // 2
     dma = pltpu.SemaphoreType.DMA
     bf16 = jnp.bfloat16
     scratch = [
@@ -305,15 +352,18 @@
         pltpu.VMEM((2, columns, 4 * count, split), bf16),
         pltpu.VMEM((2, columns, 2 * count, split), bf16),
         pltpu.VMEM((2, columns, count, split), bf16),
-        pltpu.VMEM((2, columns - 1, count, split), bf16),
+        pltpu.VMEM((2, columns - 1, count, kept), bf16),
         pltpu.VMEM((4 * count, 4 * hidden_half), jnp.float32),
         pltpu.VMEM((4 * count, 2 * hidden_half), bf16),
         pltpu.VMEM((count, width), bf16),
         dma((4,)), dma((3,)), dma((3,)), dma((columns,)), dma((columns,)),
-    ] + [dma((columns, 2)) for _ in range(10)]
+    ] + [dma((columns, 2)) for _ in range(10)] + [
+        dma((columns,)), dma((columns,)), dma((columns, 2)), dma((columns, 2)),
+        pltpu.VMEM((2, columns - 1, 4 * count, split - kept), bf16),
+    ]
     flops = 12 * experts * count * width * hidden_half
     return pl.pallas_call(
-        functools.partial(layer_kernel, nodes, columns, width, hidden_half),
+        functools.partial(layer_kernel, nodes, columns, width, hidden_half, extra),
         name="moe_layer",
         out_shape=jax.ShapeDtypeStruct((count, width), bf16),
         in_specs=[pl.BlockSpec(memory_space=pl.ANY)] * 4,

time: 175 us -> 159 us (0.909); the launches traced: 175 us -> 157 us
  Pallas kernels: 170 us -> 152 us
    pallas_call x1, Pallas kernels: 170 us -> 152 us  [by_rows(): pl.pallas_call(functools.partial(layer_kernel, nodes, columns, width, hid...]
where the time goes in v3:
time: 159 us; the launch traced here: 157 us
  Pallas kernels  152 us (96%)
  other arithmetic  2.69 us (2%)
  local copies, waits for them, and re-layouts  2.03 us (1%)
    pallas_call x1, Pallas kernels, by_rows(): pl.pallas_call(functools.partial(layer_kernel, nodes, columns, width, hid...  152 us

profile of v3, /device:TPU:10, one launch (start us, length us, event | category | flops | bytes accessed | tf_op | source)
XLA Modules:
  0.0 156.5 jit_solution(6625043288731806711)
XLA Ops:
  0.0 0.7 select_reduce_fusion
  0.7 0.1 copy.12
  0.8 0.1 copy.11
  0.9 0.1 fusion.6
  1.0 1.9 %pad_maximum_fusion.rows_ref = bf16[64,4224]{1,0:T(8,128)(2,1)} fusion(bf16[64,4096]{1,0:T(8,128)(2,1)} %param.6, bf16[64,128]{1,0:T(8,128)(2,1)S(1)} %fusion.6), kind=kLoop, calls=%fused_computation | loop fusion | flops 1081344 | bytes 1081344 | tf_op jit(solution)/shard_map/concatenate | solution.py:341
  2.9 151.8 %moe_layer.1 = bf16[64,4096]{1,0:T(8,128)(2,1)} custom-call(bf16[64,4224]{1,0:T(8,128)(2,1)} %pad_maximum_fusion.rows_ref, bf16[4096,384]{1,0:T(8,128)(2,1)} %gate_ref.1, bf16[4096,384]{1,0:T(8,128)(2,1)} %up_ref.1, bf16[384,4096]{1,0:T(8,128)(2,1)} %down_ref.1), custom_call_target="tpu_custom_call" | custom-call | flops 19327352832 | bytes 18874368 | tf_op jit(solution)/shard_map/moe_layer/pallas_call | solution.py:365
  154.7 1.9 %copy.15 = bf16[64,4096]{1,0:T(8,128)(2,1)} copy(bf16[64,4096]{1,0:T(8,128)(2,1)} %moe_layer.1) | data formatting | bytes 1048576
  (2 shorter events, 0.0 us)
